TPU v7x, 32 devices: a whole 2x2x4 slice. The times are simulated.
32 devices in a mesh: parts: 2 (over y), walk: 4 (over z), slab: 2 (over x), row: 2 (over core).
Axes of the slice: x: 2, y: 2, z: 4, core: 2. Of those that a mesh axis runs over, the one named last changes fastest.
Arguments:
- walkers: bfloat16 [64, 1024, 256], P(('parts', 'walk'), ('slab', 'row')), parts along dimension 0
- trial_orbitals: bfloat16 [2048, 256], P(('parts', 'slab', 'row')), parts along dimension 0
- cholesky: bfloat16 [16, 256, 1024], P(('parts', 'slab', 'row')), parts along dimension 0, may hold values from -0.359375 to 0.359375
- branches: int32 [64], P('parts'), parts along dimension 0, may hold values from 0 to 31, as said below
- counts: int32 [8], P(('parts', 'walk')), parts along dimension 0, may hold values from 4 to 8, as said below
- field: float32 [64, 1024], P(('parts', 'walk'), ('slab', 'row')), parts along dimension 0, may hold values from 0.7 to 1.3
Outputs:
- force_bias: float32 [64, 8], P(('parts', 'walk'), ('slab', 'row')), parts along dimension 0
- exchange_energy: float32 [64, 8], P(('parts', 'walk'), ('slab', 'row')), parts along dimension 0
There are 2 independent parts, one for each index of `parts`. A program takes and returns all parts, laid end to end along the dimension named above; each array names one. Nothing has to cross between parts.
Inputs may be any that keep to these rules, and one draw needn't show every extreme that they name: `branches`: the new walkers of one walk index copy at most 2 walkers from any one walk index, and some walk index gives exactly 2 to some walk index. `counts`: at least one walk index has all 8 alive; the alive ones are the first of its walkers.
All inputs are finite; a program needn't handle non-finite values. Where the computation divides by a largest or mean magnitude, that divisor is 1e-20 or more.
Results may differ from a plain program's by a relative error of at most 0.0068.
Values may be sent and summed in bfloat16 or wider, within the bound.
A program may use at most 64 MiB of HBM per device.

v0:
```python
import jax
import jax.numpy as jnp
from jax import lax
from jax.sharding import PartitionSpec as P

ITERS = 10


HIGHEST = lax.Precision.HIGHEST


def newton_schulz(intersection):
    column_max = jnp.max(jnp.sum(jnp.abs(intersection), axis=0))
    row_max = jnp.max(jnp.sum(jnp.abs(intersection), axis=1))
    inverse = intersection.T / (column_max * row_max)
    twice_identity = 2.0 * jnp.eye(intersection.shape[0], dtype=intersection.dtype)
    for iteration in range(ITERS):
        inverse = jnp.dot(
            inverse,
            twice_identity - jnp.dot(intersection, inverse, precision=HIGHEST),
            precision=HIGHEST,
        )
    return inverse


def on_device(walkers, trial_orbitals, cholesky, branches, counts, field):
    walk_size = lax.axis_size("walk")
    position = lax.axis_index("walk")
    per_device = walkers.shape[0]
    row_count = walkers.shape[1]
    electrons = walkers.shape[2]
    capacity = (per_device + walk_size - 1) // walk_size
    sender = branches.reshape(walk_size, per_device) // per_device
    local_index = branches.reshape(walk_size, per_device) % per_device
    same_sender = sender[:, :, None] == sender[:, None, :]
    earlier = jnp.arange(per_device)[None, :] < jnp.arange(per_device)[:, None]
    arrival_rank = jnp.sum(same_sender & earlier[None], axis=2)
    wanted = (sender[:, None, :] == position) & (
        arrival_rank[:, None, :] == jnp.arange(capacity, dtype=jnp.int32)[None, :, None]
    )
    chosen = jnp.sum(jnp.where(wanted, local_index[:, None, :], 0), axis=2).reshape(-1)
    present = jnp.any(wanted, axis=2).reshape(-1)
    outgoing = jnp.take(walkers, chosen, axis=0)
    outgoing = jnp.where(present[:, None, None], outgoing, jnp.zeros_like(outgoing))
    outgoing = outgoing.reshape(walk_size, capacity, row_count, electrons)
    arrived = lax.all_to_all(outgoing, "walk", split_axis=0, concat_axis=0, tiled=True)
    my_sender = lax.dynamic_index_in_dim(sender, position, 0, keepdims=False)
    my_rank = lax.dynamic_index_in_dim(arrival_rank, position, 0, keepdims=False)
    arrived_flat = arrived.reshape(walk_size * capacity, row_count, electrons)
    migrated = jnp.take(arrived_flat, my_sender * capacity + my_rank, axis=0)
    propagated = (migrated.astype(jnp.float32) * field[:, :, None]).astype(jnp.bfloat16)
    everything = lax.all_gather(propagated, ("slab", "row"), axis=1, tiled=True)
    shard_count = lax.axis_size(("slab", "row"))
    shard_index = lax.axis_index(("slab", "row"))
    share = per_device // shard_count
    trial_whole = lax.all_gather(trial_orbitals, ("slab", "row"), axis=0, tiled=True)
    own_walkers = lax.dynamic_slice_in_dim(everything, shard_index * share, share, 0)
    intersection = jnp.einsum(
        "mn,wmk->wnk", trial_whole, own_walkers, preferred_element_type=jnp.float32
    )
    inverse = jax.vmap(newton_schulz)(intersection).astype(jnp.bfloat16)
    inverses = lax.all_gather(inverse, ("slab", "row"), axis=0, tiled=True)
    green_full = jnp.einsum(
        "wmn,wnk->wmk", everything, inverses, preferred_element_type=jnp.float32
    ).astype(jnp.bfloat16)
    contracted = jnp.einsum(
        "gnm,wmk->wgnk", cholesky, green_full, preferred_element_type=jnp.float32
    )
    living = (jnp.arange(per_device, dtype=jnp.int32) < counts[0]).astype(jnp.float32)[:, None]
    force_bias = jnp.trace(contracted, axis1=2, axis2=3) * living
    exchange_energy = -0.5 * jnp.einsum("wgnk,wgkn->wg", contracted, contracted) * living
    return (force_bias, exchange_energy)


def solution(mesh):
    return jax.shard_map(
        on_device,
        mesh=mesh,
        in_specs=(
            P(("parts", "walk"), ("slab", "row"), None),
            P(("parts", "slab", "row"), None),
            P(("parts", "slab", "row"), None, None),
            P("parts"),
            P(("parts", "walk")),
            P(("parts", "walk"), ("slab", "row")),
        ),
        out_specs=(P(("parts", "walk"), ("slab", "row")), P(("parts", "walk"), ("slab", "row"))),
        check_vma=False,
    )
```

profile of v0, /device:TPU:1, one launch (start us, length us, event | category | flops | bytes accessed | tf_op | source)
XLA Modules:
  0.0 143.6 jit_solution(5911564659753167839)
XLA Ops:
  7.2 0.0 copy-start
  7.2 0.8 reshape.146
  8.0 0.2 convert_reduce_fusion
  8.3 0.2 select_reduce_fusion
  8.4 0.1 copy.28
  8.5 0.1 reshape.147
  8.6 0.1 fusion.17
  8.8 0.1 copy.27
  8.9 0.1 broadcast_in_dim.41
  9.0 1.8 %gather_fusion = bf16[8,256,256]{2,1,0:T(8,128)(2,1)S(1)} fusion(bf16[8,256,256]{2,1,0:T(8,128)(2,1)} %param.8, s32[1024]{0:T(1024)S(1)} %pad_clamp_fusion.1), kind=kCustom, calls=%fused_computation.clone | custom fusion | bytes 2097184 | tf_op jit(solution)/shard_map/jit(_take)/gather | solution.py:43
  10.8 0.0 copy-start.2
  10.8 1.2 select_select_fusion
  12.0 5.4 %all-to-all-start = ((bf16[4,2,256,256]{3,2,1,0:T(8,128)(2,1)}), bf16[4,2,256,256]{3,2,1,0:T(8,128)(2,1)S(1)}, u32[]{:S(2)}, u32[]{:S(2)}) async-start(bf16[4,2,256,256]{3,2,1,0:T(8,128)(2,1)} %bitcast.2), calls=%async_computation | async-start | bytes 2097152 | tf_op jit(solution)/shard_map/all_to_all | solution.py:46
  17.4 0.0 copy-start.1
  17.4 0.0 all-gather.3.cloned.1.call-start
  17.5 25.3 %all-to-all-done = bf16[4,2,256,256]{3,2,1,0:T(8,128)(2,1)S(1)} async-done(((bf16[4,2,256,256]{3,2,1,0:T(8,128)(2,1)}), bf16[4,2,256,256]{3,2,1,0:T(8,128)(2,1)S(1)}, u32[]{:S(2)}, u32[]{:S(2)}) %all-to-all-start) | async-done | bytes 1048608 | tf_op jit(solution)/shard_map/all_to_all | solution.py:46
  42.7 0.6 gather_fusion.1
  43.3 0.5 copy.29
  43.9 0.0 copy-done.2
  43.9 1.3 multiply_convert_fusion
  45.2 0.0 all-gather.3.cloned.1.call-update
  45.2 0.0 all-gather.5.cloned.1.call-start
  45.3 0.0 copy-done.1
  45.3 8.4 %all_gather.10 = bf16[1024,256]{1,0:T(8,128)(2,1)S(1)} all-gather(bf16[256,256]{1,0:T(8,128)(2,1)S(1)} %copy-done.1), channel_id=1, replica_groups=mesh['parts'=2,'walk'=4,'slab'=2,'row'=2] {'slab','row'}, dimensions={0}, use_global_device_ids=true | all-gather | bytes 655360 | tf_op jit(solution)/shard_map/all_gather | solution.py:56
  53.7 26.9 %all-gather.3.cloned.1.call-done = bf16[8,1024,256]{1,2,0:T(8,128)(2,1)} async-done(((bf16[8,256,256]{1,2,0:T(8,128)(2,1)}), bf16[8,1024,256]{1,2,0:T(8,128)(2,1)}) %all-gather.3.cloned.1.call-update) | async-done | bytes 4194320 | tf_op jit(solution)/shard_map/all_gather | solution.py:52
  80.6 1.7 %abs_reduce_fusion = (f32[2,256]{1,0:T(2,128)S(1)}, f32[2,256]{1,0:T(2,128)S(1)}, f32[2,256,256]{2,1,0:T(8,128)S(1)}) fusion(bf16[1024,256]{1,0:T(8,128)(2,1)S(1)} %all_gather.10, bf16[8,1024,256]{1,2,0:T(8,128)(2,1)} %all-gather.3.cloned.1.call-done, s32[]{:T(128)S(6)} %select_n.60), kind=kOutput, calls=%fused_computation.27 | convolution fusion | flops 268827648 | bytes 2101252 | tf_op jit(solution)/shard_map/mn,wmk->wnk/dot_general | solution.py:58
  82.3 0.1 reduce_max.18
  82.5 0.1 reduce_max.19
  82.6 1.1 convolution_subtract_fusion.9
  83.6 0.7 fusion.11
  84.3 1.0 convolution_subtract_fusion.8
  85.4 0.7 fusion.22
  86.1 1.0 convolution_subtract_fusion.7
  87.1 0.7 fusion.23
  87.8 1.0 convolution_subtract_fusion.6
  88.8 0.7 fusion.24
  89.5 1.0 convolution_subtract_fusion.5
  90.5 0.7 fusion.25
  91.2 1.0 convolution_subtract_fusion.4
  92.3 0.7 fusion.26
  92.9 1.0 convolution_subtract_fusion.3
  94.0 0.7 fusion.27
  94.6 1.2 convolution_subtract_fusion.2
  95.9 0.7 fusion.28
  96.5 1.0 convolution_subtract_fusion.1
  97.6 0.7 fusion.29
  98.2 1.0 convolution_subtract_fusion
  99.3 1.3 convolution_convert_fusion
  100.7 0.0 all-gather.5.cloned.1.call-update
  100.7 0.2 copy.26
  101.6 16.0 %all-gather.5.cloned.1.call-done = bf16[8,256,256]{2,1,0:T(8,128)(2,1)} async-done(((bf16[2,256,256]{2,1,0:T(8,128)(2,1)}), bf16[8,256,256]{2,1,0:T(8,128)(2,1)}) %all-gather.5.cloned.1.call-update) | async-done | bytes 1048592 | tf_op jit(solution)/shard_map/all_gather | solution.py:62
  117.5 0.0 copy-done
  117.5 8.1 %fusion = f32[8,256,2,256]{3,1,2,0:T(8,128)} fusion(bf16[8,1024,256]{1,2,0:T(8,128)(2,1)} %all-gather.3.cloned.1.call-done, bf16[8,256,256]{2,1,0:T(8,128)(2,1)} %all-gather.5.cloned.1.call-done, bf16[2,256,1024]{2,1,0:T(8,128)(2,1)S(1)} %copy-done), kind=kOutput, calls=%fused_computation.2 | convolution fusion | flops 3223322624 | bytes 10485760 | tf_op jit(solution)/shard_map/gnm,wmk->wgnk/dot_general | solution.py:66
  125.6 5.3 %copy.59 = f32[8,2,256,256]{2,3,1,0:T(8,128)} copy(f32[8,2,256,256]{3,2,1,0:T(8,128)} %bitcast.70) | data formatting | bytes 8388608
  131.0 4.4 %fusion.3 = (f32[8,2]{1,0:T(8,128)S(1)}, f32[8,2]{1,0:T(8,128)S(1)}) fusion(f32[8,2,256,256]{2,3,1,0:T(8,128)} %copy.59, f32[8,256,2,256]{3,1,2,0:T(8,128)} %fusion, pred[256,256]{0,1:T(8,128)(4,1)S(1)} %copy.26), kind=kLoop, calls=%fused_computation.7 | loop fusion | flops 4194272 | bytes 8454272
  135.4 0.1 broadcast_multiply_fusion
  135.5 0.6 copy.42
  136.1 0.1 copy.60
  136.2 0.6 broadcast_multiply_fusion.1
  (13 shorter events, 0.1 us)
Async XLA Ops:
  7.2 110.4 %copy-start = (bf16[2,256,1024]{2,1,0:T(8,128)(2,1)S(1)}, bf16[2,256,1024]{2,1,0:T(8,128)(2,1)}, u32[]{:S(2)}) copy-start(bf16[2,256,1024]{2,1,0:T(8,128)(2,1)} %param.10) | copy-start | bytes 3145732
  10.8 33.0 %copy-start.2 = (f32[8,256]{1,0:T(8,128)S(1)}, f32[8,256]{1,0:T(8,128)}, u32[]{:S(2)}) copy-start(f32[8,256]{1,0:T(8,128)} %param.13) | copy-start | bytes 24580
  12.0 30.7 %all-to-all-start = ((bf16[4,2,256,256]{3,2,1,0:T(8,128)(2,1)}), bf16[4,2,256,256]{3,2,1,0:T(8,128)(2,1)S(1)}, u32[]{:S(2)}, u32[]{:S(2)}) async-start(bf16[4,2,256,256]{3,2,1,0:T(8,128)(2,1)} %bitcast.2), calls=%async_computation | async-start | bytes 2097152 | tf_op jit(solution)/shard_map/all_to_all | solution.py:46
  17.4 27.9 %copy-start.1 = (bf16[256,256]{1,0:T(8,128)(2,1)S(1)}, bf16[256,256]{1,0:T(8,128)(2,1)}, u32[]{:S(2)}) copy-start(bf16[256,256]{1,0:T(8,128)(2,1)} %param.9) | copy-start | bytes 393220
  17.4 63.2 %all-gather.3.cloned.1.call-start = ((), (), s32[]{:S(2)}) async-start(), calls=%async_computation.1 | async-start | bytes 5242880 | tf_op jit(solution)/shard_map/all_gather | solution.py:52
  45.2 72.3 %all-gather.5.cloned.1.call-start = ((), (), s32[]{:S(2)}) async-start(), calls=%async_computation.2 | async-start | bytes 1310720 | tf_op jit(solution)/shard_map/all_gather | solution.py:62
Sparse Core Ops, SparseCore 0:
  45.3 35.2 all-gather.2
  100.8 16.6 all-gather.4
where the time goes:
time: 144 us
  waiting for transfers between devices  68.1 us (47%)
  matrix products  27.8 us (19%)
  between operations  15 us (10%)
  local copies, waits for them, and re-layouts  10.4 us (7%)
  blocking collectives  8.4 us (6%)
  other arithmetic  8.38 us (6%)
  starting transfers between devices  5.45 us (4%)
    all_gather x1, waiting for transfers between devices, on_device(): everything = lax.all_gather(propagated, ('slab', 'row'), axis=1, tiled=True)  26.9 us
    all_to_all x1, waiting for transfers between devices, on_device(): lax.all_to_all(outgoing, 'walk', split_axis=0, concat_axis=0, tiled=True)  25.3 us
    all_gather x1, waiting for transfers between devices, on_device(): inverses = lax.all_gather(inverse, ('slab', 'row'), axis=0, tiled=True)  16 us
    dot_general x10, matrix products, newton_schulz(): jnp.dot(intersection, inverse, precision=HIGHEST)  10.7 us
    all_gather x1, blocking collectives, on_device(): lax.all_gather(trial_orbitals, ('slab', 'row'), axis=0, tiled=True)  8.4 us
    dot_general x1, matrix products, on_device(): jnp.einsum('gnm,wmk->wgnk', cholesky, green_full, preferred_element_type=...  8.12 us
    dot_general x10, matrix products, newton_schulz(): jnp.dot(inverse, twice_identity - jnp.dot(intersection, inverse, precisio...  7.25 us
    unnamed x8, local copies, waits for them, and re-layouts  6.01 us
  transfers between devices with their start and end apart: 3, of which 3 were waited for; matrix products, arithmetic and copies ran while one was open for 0% of the time, Pallas kernels for 0%

commit v1 on v0

v1 whole, which is shorter than its diff:
```python
import functools

import jax
import jax.numpy as jnp
from jax import lax
from jax.experimental import pallas as pl
from jax.experimental.pallas import tpu as pltpu
from jax.sharding import PartitionSpec as P

ITERS = 10
MESH = pl.DeviceIdType.MESH


def split(x):
    high = x.astype(jnp.bfloat16)
    low = (x - high.astype(jnp.float32)).astype(jnp.bfloat16)
    return high, low


def dot(a, b):
    return jnp.dot(a, b, preferred_element_type=jnp.float32)


def dot3(a, b):
    ah, al = split(a)
    bh, bl = split(b)
    return dot(ah, bh) + (dot(ah, bl) + dot(al, bh))


def kernel(
    sizes, out_ref, trial_ref, chol_ref, field_ref, bias_ref, exch_ref,
    raw, trial, field, prop, half, inter, stack, inverse,
    z_send, z_recv, x_send, x_recv, c_send, c_recv, i_send, i_recv,
    tx_send, tx_recv, tc_send, tc_recv, fx_send, fx_recv, fc_send, fc_recv, own_sem,
):
    walks, slabs, cores, slots, local = sizes
    walk, slab, core = lax.axis_index("walk"), lax.axis_index("slab"), lax.axis_index("row")
    rows, electrons = trial_ref.shape[1], trial_ref.shape[0]
    vectors = chol_ref.shape[0] // electrons
    mine = slab * cores + core

    def slab_peer(step):
        return lax.rem(slab + step, slabs)

    def core_peer(step):
        return lax.rem(core + step, cores)

    def slab_source(step):
        return lax.rem(slab + slabs - step, slabs)

    def core_source(step):
        return lax.rem(core + cores - step, cores)

    barrier = pltpu.get_barrier_semaphore()
    greeted = 0
    if local < slots:
        for step in range(1, walks):
            pl.semaphore_signal(barrier, inc=1, device_id={"walk": lax.rem(walk + step, walks)}, device_id_type=MESH)
            greeted += 1
    for step in range(1, slabs):
        pl.semaphore_signal(barrier, inc=1, device_id={"slab": slab_peer(step)}, device_id_type=MESH)
        greeted += 1
    for step in range(1, cores):
        pl.semaphore_signal(barrier, inc=1, device_id={"row": core_peer(step)}, device_id_type=MESH)
        greeted += 1
    pl.semaphore_wait(barrier, greeted)

    def remote(src, dst, send, recv, target):
        return pltpu.make_async_remote_copy(
            src_ref=src, dst_ref=dst, send_sem=send, recv_sem=recv, device_id=target, device_id_type=MESH
        )

    def z_copy(i, step):
        return remote(out_ref.at[i], raw.at[i, mine], z_send.at[i], z_recv.at[i], {"walk": lax.rem(walk + step, walks)})

    def x_copy(i, step):
        return remote(raw.at[i, mine], raw.at[i, mine], x_send.at[step, i], x_recv.at[step, i], {"slab": slab_peer(step)})

    def c_copy(i, hop, step):
        q = slab_source(hop) * cores + core
        return remote(raw.at[i, q], raw.at[i, q], c_send.at[hop, step, i], c_recv.at[hop, step, i], {"row": core_peer(step)})

    def small(src, buf, xs, xr, cs, cr):
        def x(step):
            return remote(src, buf.at[mine], xs.at[step], xr.at[step], {"slab": slab_peer(step)})

        def c(hop, step):
            q = slab_source(hop) * cores + core
            block = src if hop == 0 else buf.at[q]
            return remote(block, buf.at[q], cs.at[hop, step], cr.at[hop, step], {"row": core_peer(step)})

        return x, c

    own = [pltpu.make_async_copy(out_ref.at[i], raw.at[i, mine], own_sem.at[i]) for i in range(local)]
    own.append(pltpu.make_async_copy(trial_ref, trial.at[mine], own_sem.at[local]))
    own.append(pltpu.make_async_copy(field_ref, field.at[mine], own_sem.at[local + 1]))
    for copy in own:
        copy.start()
    for i in range(local, slots):
        z_copy(i, i // local).start()
    pairs = [
        small(trial_ref, trial, tx_send, tx_recv, tc_send, tc_recv),
        small(field_ref, field, fx_send, fx_recv, fc_send, fc_recv),
    ]
    for x, c in pairs:
        for step in range(1, slabs):
            x(step).start()
        for step in range(1, cores):
            c(0, step).start()
    for copy in own:
        copy.wait()

    def spread(i):
        for step in range(1, slabs):
            x_copy(i, step).start()
        for step in range(1, cores):
            c_copy(i, 0, step).start()

    def relay(i):
        for hop in range(1, slabs):
            x_copy(i, hop).wait_recv()
            for step in range(1, cores):
                c_copy(i, hop, step).start()

    def compute(i):
        for hop in range(slabs):
            for step in range(1, cores):
                c_copy(i, hop, step).wait_recv()
        for q in range(slabs * cores):
            column = jnp.transpose(field[q])
            lane = lax.broadcasted_iota(jnp.int32, column.shape, 1)
            scale = jnp.sum(jnp.where(lane == i, column, 0.0), axis=1, keepdims=True)
            prop[q * rows : (q + 1) * rows, :] = (raw[i, q].astype(jnp.float32) * scale).astype(jnp.bfloat16)
        half[i] = dot(chol_ref[...], prop[...]).astype(jnp.bfloat16)

        @pl.when(lax.rem(i, cores) == core)
        def _():
            total = dot(trial[0], prop[0:rows, :])
            for q in range(1, slabs * cores):
                total += dot(trial[q], prop[q * rows : (q + 1) * rows, :])
            inter[i // cores] = total

    for i in range(local):
        spread(i)
    for x, c in pairs:
        for hop in range(1, slabs):
            x(hop).wait_recv()
            for step in range(1, cores):
                c(hop, step).start()
    for x, c in pairs:
        for hop in range(slabs):
            for step in range(1, cores):
                c(hop, step).wait_recv()

    @pl.loop(0, slots + 2)
    def _(i):
        @pl.when((i >= local) & (i < slots))
        def _():
            z_copy(i, 0).wait_recv()
            spread(i)

        @pl.when((i > 0) & (i <= slots))
        def _():
            relay(i - 1)

        @pl.when(i > 1)
        def _():
            compute(i - 2)

    share = slots // cores
    for n in range(share):
        matrix = inter[n]
        sizes_of = jnp.abs(matrix)
        column_max = jnp.max(jnp.sum(sizes_of, axis=0, keepdims=True), axis=1, keepdims=True)
        row_max = jnp.max(jnp.sum(sizes_of, axis=1, keepdims=True), axis=0, keepdims=True)
        start = jnp.transpose(matrix) / (column_max * row_max)
        stack[n, 0:electrons, :] = start
        stack[n, electrons:, :] = dot3(matrix, start)

    @pl.loop(0, ITERS)
    def _(iteration):
        for n in range(share):
            both = stack[n]
            stack[n] = 2.0 * both - dot3(both, both[electrons:, :])

    def i_copy(n, c, step):
        place = inverse.at[n * cores + c]
        return remote(place, place, i_send.at[n, step], i_recv.at[n, step], {"row": core_peer(step)})

    for n in range(share):
        inverse[n * cores + core] = stack[n, 0:electrons, :].astype(jnp.bfloat16)
        for step in range(1, cores):
            i_copy(n, core, step).start()
    for n in range(share):
        for step in range(1, cores):
            i_copy(n, core_source(step), step).wait_recv()

    line = lax.broadcasted_iota(jnp.int32, (electrons, electrons), 0)
    diagonal = line == lax.broadcasted_iota(jnp.int32, (electrons, electrons), 1)

    @pl.loop(0, slots)
    def _(i):
        contracted = dot(half[i], inverse[i])
        for g in range(vectors):
            block = contracted[g * electrons : (g + 1) * electrons, :]
            bias_ref[i, g : g + 1, :] = jnp.sum(jnp.where(diagonal, block, 0.0), axis=0, keepdims=True)
            exch_ref[i, g : g + 1, :] = jnp.sum(block * jnp.transpose(block), axis=0, keepdims=True)

    for i in range(local, slots):
        z_copy(i, i // local).wait_send()

    @pl.loop(0, slots)
    def _(i):
        for step in range(1, slabs):
            x_copy(i, step).wait_send()
        for hop in range(slabs):
            for step in range(1, cores):
                c_copy(i, hop, step).wait_send()

    for x, c in pairs:
        for step in range(1, slabs):
            x(step).wait_send()
        for hop in range(slabs):
            for step in range(1, cores):
                c(hop, step).wait_send()
    for n in range(share):
        for step in range(1, cores):
            i_copy(n, core, step).wait_send()


def on_device(walkers, trial_orbitals, cholesky, branches, counts, field):
    walks, slabs, cores = lax.axis_size("walk"), lax.axis_size("slab"), lax.axis_size("row")
    walk = lax.axis_index("walk")
    per_device, rows, electrons = walkers.shape
    vectors = cholesky.shape[0]
    capacity = (per_device + walks - 1) // walks
    sender = branches.reshape(walks, per_device) // per_device
    local_index = branches.reshape(walks, per_device) % per_device
    places = jnp.arange(per_device, dtype=jnp.int32)
    same_sender = sender[:, :, None] == sender[:, None, :]
    rank = jnp.sum(same_sender & (places[None, :] < places[:, None])[None], axis=2)
    my_sender = lax.dynamic_index_in_dim(sender, walk, 0, keepdims=False)
    my_rank = lax.dynamic_index_in_dim(rank, walk, 0, keepdims=False)
    full = walks * capacity == per_device
    wanted = (sender[:, None, :] == walk) & (rank[:, None, :] == jnp.arange(capacity, dtype=jnp.int32)[None, :, None])
    chosen = jnp.sum(jnp.where(wanted, local_index[:, None, :], 0), axis=2)
    if full:
        steps = jnp.arange(walks, dtype=jnp.int32)
        order = (walk + steps) % walks
        chosen = jnp.sum(jnp.where(order[:, None, None] == steps[None, :, None], chosen[None], 0), axis=1)
        outgoing = jnp.take(walkers, chosen.reshape(-1), axis=0, mode="clip")
        slot = ((walk - my_sender) % walks) * capacity + my_rank
        local = capacity
    else:
        outgoing = jnp.take(walkers, chosen.reshape(-1), axis=0, mode="clip")
        outgoing = outgoing.reshape(walks, capacity, rows, electrons)
        arrived = lax.all_to_all(outgoing, "walk", split_axis=0, concat_axis=0, tiled=True)
        arrived = arrived.reshape(walks * capacity, rows, electrons)
        outgoing = jnp.take(arrived, my_sender * capacity + my_rank, axis=0, mode="clip")
        slot = places
        local = per_device
    here = slot[:, None] == places[None, :]
    slot_field = jnp.sum(jnp.where(here[:, :, None], field[:, None, :], 0.0), axis=0)
    shards = slabs * cores
    share = per_device // cores
    dma = pltpu.SemaphoreType.DMA
    vmem = pl.BlockSpec(memory_space=pltpu.VMEM)
    bias, exchange = pl.pallas_call(
        functools.partial(kernel, (walks, slabs, cores, per_device, local)),
        out_shape=[jax.ShapeDtypeStruct((per_device, vectors, electrons), jnp.float32)] * 2,
        in_specs=[vmem] * 4,
        out_specs=[vmem] * 2,
        scratch_shapes=[
            pltpu.VMEM((per_device, shards, rows, electrons), jnp.bfloat16),
            pltpu.VMEM((shards, electrons, rows), jnp.bfloat16),
            pltpu.VMEM((shards, per_device, rows), jnp.float32),
            pltpu.VMEM((shards * rows, electrons), jnp.bfloat16),
            pltpu.VMEM((per_device, vectors * electrons, electrons), jnp.bfloat16),
            pltpu.VMEM((share, electrons, electrons), jnp.float32),
            pltpu.VMEM((share, 2 * electrons, electrons), jnp.float32),
            pltpu.VMEM((per_device, electrons, electrons), jnp.bfloat16),
            dma((per_device,)), dma((per_device,)),
            dma((slabs, per_device)), dma((slabs, per_device)),
            dma((slabs, cores, per_device)), dma((slabs, cores, per_device)),
            dma((share, cores)), dma((share, cores)),
            dma((slabs,)), dma((slabs,)), dma((slabs, cores)), dma((slabs, cores)),
            dma((slabs,)), dma((slabs,)), dma((slabs, cores)), dma((slabs, cores)),
            dma((local + 2,)),
        ],
        compiler_params=pltpu.CompilerParams(
            collective_id=0, has_side_effects=True, vmem_limit_bytes=48 * 1024 * 1024
        ),
    )(outgoing, trial_orbitals.T, cholesky.reshape(vectors * electrons, shards * rows), slot_field)
    living = (places < counts[0]).astype(jnp.float32)[:, None]
    bias = jnp.sum(jnp.where(here[:, :, None], jnp.sum(bias, axis=2)[None], 0.0), axis=1)
    exchange = jnp.sum(jnp.where(here[:, :, None], jnp.sum(exchange, axis=2)[None], 0.0), axis=1)
    return bias * living, -0.5 * exchange * living


def solution(mesh):
    return jax.shard_map(
        on_device,
        mesh=mesh,
        in_specs=(
            P(("parts", "walk"), ("slab", "row"), None),
            P(("parts", "slab", "row"), None),
            P(("parts", "slab", "row"), None, None),
            P("parts"),
            P(("parts", "walk")),
            P(("parts", "walk"), ("slab", "row")),
        ),
        out_specs=(P(("parts", "walk"), ("slab", "row")), P(("parts", "walk"), ("slab", "row"))),
        check_vma=False,
    )
```

time: 144 us -> 63.5 us (0.44)
  the two profiles are of different devices: /device:TPU:1 before, /device:TPU:25 now
where the time goes in v1:
time: 63.5 us; the launch traced here: 63.3 us
  Pallas kernels  57.4 us (90%)
  local copies, waits for them, and re-layouts  2.82 us (4%)
  other arithmetic  1.64 us (3%)
  between operations  1.41 us (2%)
    pallas_call x1, Pallas kernels, on_device(): pl.pallas_call(functools.partial(kernel, (walks, slabs, cores, per_device...  57.4 us
    unnamed x11, local copies, waits for them, and re-layouts  1.77 us

profile of v1, /device:TPU:25, one launch (start us, length us, event | category | flops | bytes accessed | tf_op | source)
XLA Modules:
  0.0 63.3 jit_solution(7100517950547456481)
XLA Ops:
  0.6 0.0 copy-start
  0.6 0.0 copy-start.4
  0.7 0.7 %copy-done.4 = s32[32]{0:T(128)S(1)} copy-done((s32[32]{0:T(128)S(1)}, s32[32]{0:T(128)}, u32[]{:S(2)}) %copy-start.4) | copy-done | bytes 152
  1.4 0.1 reshape.206
  1.5 0.0 copy-start.3
  1.5 0.2 convert_reduce_fusion
  1.8 0.1 iota_compare_fusion.1
  1.8 0.4 copy-done.3
  2.2 0.1 select_reduce_fusion.field_ref
  2.3 0.1 select_reduce_fusion.4
  2.4 0.1 iota_compare_fusion.3
  2.5 0.2 select_reduce_fusion.3
  2.7 0.1 copy.12
  2.8 0.1 reshape.210
  2.9 0.0 copy-done
  2.9 0.0 copy-start.2
  2.9 0.0 copy-start.1
  2.9 0.6 gather_fusion
  3.5 0.3 copy-done.2
  3.8 0.1 copy.13
  3.9 0.3 copy-done.1
  4.2 57.4 %shard_map.77 = (f32[8,2,256]{2,1,0:T(2,128)S(1)}, f32[8,2,256]{2,1,0:T(2,128)S(1)}) custom-call(bf16[8,256,256]{2,1,0:T(8,128)(2,1)S(1)} %gather_fusion, bf16[256,256]{1,0:T(8,128)(2,1)S(1)} %bitcast.10, bf16[512,1024]{1,0:T(8,128)(2,1)S(1)} %bitcast.9, f32[8,256]{1,0:T(8,128)S(1)} %select_reduce_fusion.field_ref), custom_call_target="tpu_custom_call" | custom-call | tf_op jit(solution)/shard_map/pallas_call | solution.py:268
  61.6 0.1 reduce_sum.76
  61.7 0.1 copy.14
  61.8 0.1 reduce_sum.78
  61.9 0.1 copy.15
  61.9 0.1 select_reduce_fusion.1
  62.7 0.6 broadcast_multiply_fusion
  (8 shorter events, 0.1 us)
Async XLA Ops:
  0.6 2.2 %copy-start = (bf16[8,256,256]{2,1,0:T(8,128)(2,1)S(1)}, bf16[8,256,256]{2,1,0:T(8,128)(2,1)}, u32[]{:S(2)}) copy-start(bf16[8,256,256]{2,1,0:T(8,128)(2,1)} %param.6) | copy-start | bytes 3145732
  0.6 0.7 %copy-start.4 = (s32[32]{0:T(128)S(1)}, s32[32]{0:T(128)}, u32[]{:S(2)}) copy-start(s32[32]{0:T(128)} %param.9) | copy-start | bytes 388
  1.5 0.7 %copy-start.3 = (f32[8,256]{1,0:T(8,128)S(1)}, f32[8,256]{1,0:T(8,128)}, u32[]{:S(2)}) copy-start(f32[8,256]{1,0:T(8,128)} %param.11) | copy-start | bytes 24580
  2.9 0.9 %copy-start.2 = (bf16[256,256]{1,0:T(8,128)(2,1)S(1)}, bf16[256,256]{1,0:T(8,128)(2,1)}, u32[]{:S(2)}) copy-start(bf16[256,256]{1,0:T(8,128)(2,1)} %param.7) | copy-start | bytes 393220
  2.9 1.3 %copy-start.1 = (bf16[2,256,1024]{2,1,0:T(8,128)(2,1)S(1)}, bf16[2,256,1024]{2,1,0:T(8,128)(2,1)}, u32[]{:S(2)}) copy-start(bf16[2,256,1024]{2,1,0:T(8,128)(2,1)} %param.8) | copy-start | bytes 3145732

commit v2 on v1

--- a/solution.py
+++ b/solution.py
@@ -27,9 +27,20 @@
     return dot(ah, bh) + (dot(ah, bl) + dot(al, bh))
 
 
+def partner(position, step, size):
+    if size & (size - 1):
+        return (position + step) % size
+    result, bit = 0, 1
+    while bit < size:
+        digit = (position // bit) % 2
+        result += bit * (1 - digit if step & bit else digit)
+        bit *= 2
+    return result
+
+
 def kernel(
     sizes, out_ref, trial_ref, chol_ref, field_ref, bias_ref, exch_ref,
-    raw, trial, field, prop, half, inter, stack, inverse,
+    raw, trial, field, chol, prop, half, inter, stack, inverse,
     z_send, z_recv, x_send, x_recv, c_send, c_recv, i_send, i_recv,
     tx_send, tx_recv, tc_send, tc_recv, fx_send, fx_recv, fc_send, fc_recv, own_sem,
 ):
@@ -51,11 +62,17 @@
     def core_source(step):
         return lax.rem(core + cores - step, cores)
 
+    own = [pltpu.make_async_copy(out_ref.at[i], raw.at[i, mine], own_sem.at[i]) for i in range(local)]
+    own.append(pltpu.make_async_copy(trial_ref, trial.at[mine], own_sem.at[local]))
+    own.append(pltpu.make_async_copy(field_ref, field.at[mine], own_sem.at[local + 1]))
+    own.append(pltpu.make_async_copy(chol_ref, chol, own_sem.at[local + 2]))
+    for copy in own:
+        copy.start()
     barrier = pltpu.get_barrier_semaphore()
     greeted = 0
     if local < slots:
         for step in range(1, walks):
-            pl.semaphore_signal(barrier, inc=1, device_id={"walk": lax.rem(walk + step, walks)}, device_id_type=MESH)
+            pl.semaphore_signal(barrier, inc=1, device_id={"walk": partner(walk, step, walks)}, device_id_type=MESH)
             greeted += 1
     for step in range(1, slabs):
         pl.semaphore_signal(barrier, inc=1, device_id={"slab": slab_peer(step)}, device_id_type=MESH)
@@ -71,7 +88,7 @@
         )
 
     def z_copy(i, step):
-        return remote(out_ref.at[i], raw.at[i, mine], z_send.at[i], z_recv.at[i], {"walk": lax.rem(walk + step, walks)})
+        return remote(out_ref.at[i], raw.at[i, mine], z_send.at[i], z_recv.at[i], {"walk": partner(walk, step, walks)})
 
     def x_copy(i, step):
         return remote(raw.at[i, mine], raw.at[i, mine], x_send.at[step, i], x_recv.at[step, i], {"slab": slab_peer(step)})
@@ -91,11 +108,6 @@
 
         return x, c
 
-    own = [pltpu.make_async_copy(out_ref.at[i], raw.at[i, mine], own_sem.at[i]) for i in range(local)]
-    own.append(pltpu.make_async_copy(trial_ref, trial.at[mine], own_sem.at[local]))
-    own.append(pltpu.make_async_copy(field_ref, field.at[mine], own_sem.at[local + 1]))
-    for copy in own:
-        copy.start()
     for i in range(local, slots):
         z_copy(i, i // local).start()
     pairs = [
@@ -131,7 +143,7 @@
             lane = lax.broadcasted_iota(jnp.int32, column.shape, 1)
             scale = jnp.sum(jnp.where(lane == i, column, 0.0), axis=1, keepdims=True)
             prop[q * rows : (q + 1) * rows, :] = (raw[i, q].astype(jnp.float32) * scale).astype(jnp.bfloat16)
-        half[i] = dot(chol_ref[...], prop[...]).astype(jnp.bfloat16)
+        half[i] = dot(chol[...], prop[...]).astype(jnp.bfloat16)
 
         @pl.when(lax.rem(i, cores) == core)
         def _():
@@ -152,60 +164,73 @@
             for step in range(1, cores):
                 c(hop, step).wait_recv()
 
-    @pl.loop(0, slots + 2)
-    def _(i):
-        @pl.when((i >= local) & (i < slots))
-        def _():
-            z_copy(i, 0).wait_recv()
-            spread(i)
-
-        @pl.when((i > 0) & (i <= slots))
-        def _():
-            relay(i - 1)
-
-        @pl.when(i > 1)
-        def _():
-            compute(i - 2)
-
     share = slots // cores
-    for n in range(share):
+    line = lax.broadcasted_iota(jnp.int32, (electrons, electrons), 0)
+    diagonal = line == lax.broadcasted_iota(jnp.int32, (electrons, electrons), 1)
+
+    def i_copy(i, step):
+        place = inverse.at[i]
+        return remote(place, place, i_send.at[i // cores, step], i_recv.at[i // cores, step], {"row": core_peer(step)})
+
+    def first_guess(n):
         matrix = inter[n]
         sizes_of = jnp.abs(matrix)
         column_max = jnp.max(jnp.sum(sizes_of, axis=0, keepdims=True), axis=1, keepdims=True)
         row_max = jnp.max(jnp.sum(sizes_of, axis=1, keepdims=True), axis=0, keepdims=True)
         start = jnp.transpose(matrix) / (column_max * row_max)
-        stack[n, 0:electrons, :] = start
-        stack[n, electrons:, :] = dot3(matrix, start)
-
-    @pl.loop(0, ITERS)
-    def _(iteration):
-        for n in range(share):
-            both = stack[n]
-            stack[n] = 2.0 * both - dot3(both, both[electrons:, :])
-
-    def i_copy(n, c, step):
-        place = inverse.at[n * cores + c]
-        return remote(place, place, i_send.at[n, step], i_recv.at[n, step], {"row": core_peer(step)})
-
-    for n in range(share):
-        inverse[n * cores + core] = stack[n, 0:electrons, :].astype(jnp.bfloat16)
-        for step in range(1, cores):
-            i_copy(n, core, step).start()
-    for n in range(share):
-        for step in range(1, cores):
-            i_copy(n, core_source(step), step).wait_recv()
-
-    line = lax.broadcasted_iota(jnp.int32, (electrons, electrons), 0)
-    diagonal = line == lax.broadcasted_iota(jnp.int32, (electrons, electrons), 1)
-
-    @pl.loop(0, slots)
-    def _(i):
+        stack[0:electrons, :] = start
+        stack[electrons:, :] = dot3(matrix, start)
+
+    def finish(i):
+        @pl.when(lax.rem(i, cores) != core)
+        def _():
+            i_copy(i, lax.rem(core + cores - lax.rem(i, cores), cores)).wait_recv()
+
         contracted = dot(half[i], inverse[i])
         for g in range(vectors):
             block = contracted[g * electrons : (g + 1) * electrons, :]
             bias_ref[i, g : g + 1, :] = jnp.sum(jnp.where(diagonal, block, 0.0), axis=0, keepdims=True)
             exch_ref[i, g : g + 1, :] = jnp.sum(block * jnp.transpose(block), axis=0, keepdims=True)
 
+    ready = cores + 1
+
+    @pl.loop(0, slots + ready + cores)
+    def _(i):
+        @pl.when((i >= local) & (i < slots))
+        def _():
+            z_copy(i, 0).wait_recv()
+            spread(i)
+
+        @pl.when((i > 0) & (i <= slots))
+        def _():
+            relay(i - 1)
+
+        @pl.when((i > 1) & (i < slots + 2))
+        def _():
+            compute(i - 2)
+
+        for part in range(cores):
+
+            @pl.when((i >= ready) & (i < slots + ready) & (lax.rem(i + cores - 1, cores) == part))
+            def _():
+                n = (i - ready) // cores
+                if part == 0:
+                    first_guess(n)
+
+                @pl.loop(ITERS * part // cores, ITERS * (part + 1) // cores)
+                def _(iteration):
+                    both = stack[...]
+                    stack[...] = 2.0 * both - dot3(both, both[electrons:, :])
+
+                if part == cores - 1:
+                    inverse[n * cores + core] = stack[0:electrons, :].astype(jnp.bfloat16)
+                    for step in range(1, cores):
+                        i_copy(n * cores + core, step).start()
+
+        @pl.when(i >= ready + cores)
+        def _():
+            finish(i - ready - cores)
+
     for i in range(local, slots):
         z_copy(i, i // local).wait_send()
 
@@ -225,7 +250,7 @@
                 c(hop, step).wait_send()
     for n in range(share):
         for step in range(1, cores):
-            i_copy(n, core, step).wait_send()
+            i_copy(n * cores + core, step).wait_send()
 
 
 def on_device(walkers, trial_orbitals, cholesky, branches, counts, field):
@@ -246,10 +271,12 @@
     chosen = jnp.sum(jnp.where(wanted, local_index[:, None, :], 0), axis=2)
     if full:
         steps = jnp.arange(walks, dtype=jnp.int32)
-        order = (walk + steps) % walks
+        order = jnp.stack([partner(walk, step, walks) for step in range(walks)])
+        origin = order if walks & (walks - 1) == 0 else (walk - steps) % walks
         chosen = jnp.sum(jnp.where(order[:, None, None] == steps[None, :, None], chosen[None], 0), axis=1)
         outgoing = jnp.take(walkers, chosen.reshape(-1), axis=0, mode="clip")
-        slot = ((walk - my_sender) % walks) * capacity + my_rank
+        step_of = jnp.sum(jnp.where(my_sender[:, None] == origin[None, :], steps[None, :], 0), axis=1)
+        slot = step_of * capacity + my_rank
         local = capacity
     else:
         outgoing = jnp.take(walkers, chosen.reshape(-1), axis=0, mode="clip")
@@ -268,16 +295,17 @@
     bias, exchange = pl.pallas_call(
         functools.partial(kernel, (walks, slabs, cores, per_device, local)),
         out_shape=[jax.ShapeDtypeStruct((per_device, vectors, electrons), jnp.float32)] * 2,
-        in_specs=[vmem] * 4,
+        in_specs=[pl.BlockSpec(memory_space=pl.ANY)] * 4,
         out_specs=[vmem] * 2,
         scratch_shapes=[
             pltpu.VMEM((per_device, shards, rows, electrons), jnp.bfloat16),
             pltpu.VMEM((shards, electrons, rows), jnp.bfloat16),
             pltpu.VMEM((shards, per_device, rows), jnp.float32),
+            pltpu.VMEM((vectors * electrons, shards * rows), jnp.bfloat16),
             pltpu.VMEM((shards * rows, electrons), jnp.bfloat16),
             pltpu.VMEM((per_device, vectors * electrons, electrons), jnp.bfloat16),
             pltpu.VMEM((share, electrons, electrons), jnp.float32),
-            pltpu.VMEM((share, 2 * electrons, electrons), jnp.float32),
+            pltpu.VMEM((2 * electrons, electrons), jnp.float32),
             pltpu.VMEM((per_device, electrons, electrons), jnp.bfloat16),
             dma((per_device,)), dma((per_device,)),
             dma((slabs, per_device)), dma((slabs, per_device)),
@@ -285,7 +313,7 @@
             dma((share, cores)), dma((share, cores)),
             dma((slabs,)), dma((slabs,)), dma((slabs, cores)), dma((slabs, cores)),
             dma((slabs,)), dma((slabs,)), dma((slabs, cores)), dma((slabs, cores)),
-            dma((local + 2,)),
+            dma((local + 3,)),
         ],
         compiler_params=pltpu.CompilerParams(
             collective_id=0, has_side_effects=True, vmem_limit_bytes=48 * 1024 * 1024

time: 63.5 us -> 56.8 us (0.89)
  the two profiles are of different devices: /device:TPU:25 before, /device:TPU:1 now
where the time goes in v2:
time: 56.8 us; the launch traced here: 55.9 us
  Pallas kernels  50.3 us (89%)
  local copies, waits for them, and re-layouts  2.33 us (4%)
  other arithmetic  1.79 us (3%)
  between operations  1.45 us (3%)
    pallas_call x1, Pallas kernels, on_device(): pl.pallas_call(functools.partial(kernel, (walks, slabs, cores, per_device...  50.3 us
    unnamed x11, local copies, waits for them, and re-layouts  1.27 us

profile of v2, /device:TPU:1, one launch (start us, length us, event | category | flops | bytes accessed | tf_op | source)
XLA Modules:
  0.0 55.9 jit_solution(744076602011929848)
XLA Ops:
  0.6 0.0 copy-start
  0.7 0.1 pad_add_fusion
  0.8 0.0 copy-start.4
  0.8 0.1 iota_compare_fusion.3
  0.8 0.6 %copy-done.4 = s32[32]{0:T(128)S(1)} copy-done((s32[32]{0:T(128)S(1)}, s32[32]{0:T(128)}, u32[]{:S(2)}) %copy-start.4) | copy-done | bytes 152
  1.5 0.1 reshape.179
  1.6 0.2 convert_reduce_fusion
  1.8 0.1 select_reduce_fusion.4
  2.0 0.2 select_reduce_fusion.3
  2.1 0.1 copy.12
  2.2 0.1 reshape.183
  2.3 0.0 copy-done
  2.3 0.0 copy-start.2
  2.3 0.0 copy-start.1
  2.3 0.6 %gather_fusion = bf16[8,256,256]{2,1,0:T(8,128)(2,1)S(1)} fusion(bf16[8,256,256]{2,1,0:T(8,128)(2,1)S(1)} %copy-done, s32[1024]{0:T(1024)S(1)} %pad_clamp_fusion), kind=kCustom, calls=%fused_computation | custom fusion | bytes 2097184 | tf_op jit(solution)/shard_map/jit(_take)/gather | solution.py:277
  3.0 0.0 copy-start.3
  3.0 0.1 select_reduce_fusion.5
  3.1 0.1 iota_compare_fusion.1
  3.2 0.5 copy-done.3
  3.7 0.1 select_reduce_fusion.field_ref
  3.8 0.0 copy-done.2
  3.8 0.1 copy.13
  3.9 0.0 copy-done.1
  3.9 50.3 %shard_map.77 = (f32[8,2,256]{2,1,0:T(2,128)S(1)}, f32[8,2,256]{2,1,0:T(2,128)S(1)}) custom-call(bf16[8,256,256]{2,1,0:T(8,128)(2,1)S(1)} %gather_fusion, bf16[256,256]{1,0:T(8,128)(2,1)S(1)} %bitcast.14, bf16[512,1024]{1,0:T(8,128)(2,1)S(1)} %bitcast.13, f32[8,256]{1,0:T(8,128)S(1)} %select_reduce_fusion.field_ref), custom_call_target="tpu_custom_call" | custom-call | tf_op jit(solution)/shard_map/pallas_call | solution.py:295
  54.2 0.1 reduce_sum.86
  54.3 0.1 copy.14
  54.4 0.1 reduce_sum.88
  54.5 0.1 copy.15
  54.6 0.1 select_reduce_fusion.1
  55.3 0.6 %broadcast_multiply_fusion = (f32[8,2]{0,1:T(2,128)}, f32[8,2]{0,1:T(2,128)}) fusion(f32[8,2]{0,1:T(2,128)S(1)} %get-tuple-element.6, f32[8]{0:T(128)S(1)} %compare_select_fusion, f32[8,2]{0,1:T(2,128)S(1)} %get-tuple-element.7, f32[8]{0:T(128)S(1)} %compare_convert_fusion), kind=kLoop, calls=%fused_computation.27 | loop fusion | flops 32 | bytes 320 | tf_op jit(solution)/shard_map/mul | solution.py:325
  (8 shorter events, 0.1 us)
Async XLA Ops:
  0.6 1.7 %copy-start = (bf16[8,256,256]{2,1,0:T(8,128)(2,1)S(1)}, bf16[8,256,256]{2,1,0:T(8,128)(2,1)}, u32[]{:S(2)}) copy-start(bf16[8,256,256]{2,1,0:T(8,128)(2,1)} %param.6) | copy-start | bytes 3145732
  0.8 0.7 %copy-start.4 = (s32[32]{0:T(128)S(1)}, s32[32]{0:T(128)}, u32[]{:S(2)}) copy-start(s32[32]{0:T(128)} %param.9) | copy-start | bytes 388
  2.3 1.4 %copy-start.2 = (bf16[256,256]{1,0:T(8,128)(2,1)S(1)}, bf16[256,256]{1,0:T(8,128)(2,1)}, u32[]{:S(2)}) copy-start(bf16[256,256]{1,0:T(8,128)(2,1)} %param.7) | copy-start | bytes 393220
  2.3 1.5 %copy-start.1 = (bf16[2,256,1024]{2,1,0:T(8,128)(2,1)S(1)}, bf16[2,256,1024]{2,1,0:T(8,128)(2,1)}, u32[]{:S(2)}) copy-start(bf16[2,256,1024]{2,1,0:T(8,128)(2,1)} %param.8) | copy-start | bytes 3145732
  3.0 0.7 %copy-start.3 = (f32[8,256]{1,0:T(8,128)S(1)}, f32[8,256]{1,0:T(8,128)}, u32[]{:S(2)}) copy-start(f32[8,256]{1,0:T(8,128)} %param.11) | copy-start | bytes 24580

commit v3 on v2

--- a/solution.py
+++ b/solution.py
@@ -8,6 +8,7 @@
 from jax.sharding import PartitionSpec as P
 
 ITERS = 10
+EARLY = 4
 MESH = pl.DeviceIdType.MESH
 
 
@@ -39,8 +40,8 @@
 
 
 def kernel(
-    sizes, out_ref, trial_ref, chol_ref, field_ref, bias_ref, exch_ref,
-    raw, trial, field, chol, prop, half, inter, stack, inverse,
+    sizes, branch_ref, count_ref, walker_ref, trial_ref, chol_ref, field_ref, bias_ref, exch_ref,
+    source, outgoing, field_in, field_out, traces, squares, bias_rows, exch_rows, raw, trial, field, chol, prop, half, inter, stack, inverse,
     z_send, z_recv, x_send, x_recv, c_send, c_recv, i_send, i_recv,
     tx_send, tx_recv, tc_send, tc_recv, fx_send, fx_recv, fc_send, fc_recv, own_sem,
 ):
@@ -62,10 +63,8 @@
     def core_source(step):
         return lax.rem(core + cores - step, cores)
 
-    own = [pltpu.make_async_copy(out_ref.at[i], raw.at[i, mine], own_sem.at[i]) for i in range(local)]
-    own.append(pltpu.make_async_copy(trial_ref, trial.at[mine], own_sem.at[local]))
-    own.append(pltpu.make_async_copy(field_ref, field.at[mine], own_sem.at[local + 1]))
-    own.append(pltpu.make_async_copy(chol_ref, chol, own_sem.at[local + 2]))
+    loads = [(walker_ref, source), (field_ref, field_in), (trial_ref, trial.at[mine]), (chol_ref, chol)]
+    own = [pltpu.make_async_copy(src, dst, own_sem.at[k]) for k, (src, dst) in enumerate(loads)]
     for copy in own:
         copy.start()
     barrier = pltpu.get_barrier_semaphore()
@@ -80,6 +79,50 @@
     for step in range(1, cores):
         pl.semaphore_signal(barrier, inc=1, device_id={"row": core_peer(step)}, device_id_type=MESH)
         greeted += 1
+
+    def sender(w, k):
+        return lax.div(branch_ref[w * slots + k], slots)
+
+    def kth(w, origin, values):
+        picks, count = [jnp.int32(0)] * local, jnp.int32(0)
+        for k in range(slots):
+            hit = sender(w, k) == origin
+            picks = [jnp.where(hit & (count == place), values(k), pick) for place, pick in enumerate(picks)]
+            count = count + jnp.where(hit, 1, 0)
+        return picks
+
+    for copy in own[:2]:
+        copy.wait()
+    slot_of = list(range(slots))
+    if local < slots:
+        origins = []
+        for step in range(walks):
+            target = partner(walk, step, walks)
+            picks = kth(target, walk, lambda k: lax.rem(branch_ref[target * slots + k], slots))
+            for place, pick in enumerate(picks):
+                if step == 0:
+                    raw[place, mine] = source[pick]
+                else:
+                    outgoing[step * local + place] = source[pick]
+            origin = target if walks & (walks - 1) == 0 else (walk + walks - step) % walks
+            origins.append(origin)
+            for place, pick in enumerate(kth(walk, origin, lambda k: k)):
+                i = step * local + place
+                field_out[i : i + 1, :] = field_in[pl.ds(pick, 1), :]
+        for j in range(slots):
+            origin, rank, step_of = sender(walk, j), jnp.int32(0), jnp.int32(0)
+            for k in range(j):
+                rank = rank + jnp.where(sender(walk, k) == origin, 1, 0)
+            for step in range(walks):
+                step_of = jnp.where(origins[step] == origin, step, step_of)
+            slot_of[j] = jnp.minimum(step_of * local + rank, slots - 1)
+    else:
+        for i in range(slots):
+            raw[i, mine] = source[i]
+        field_out[...] = field_in[...]
+    field[mine] = field_out[...]
+    for copy in own[2:]:
+        copy.wait()
     pl.semaphore_wait(barrier, greeted)
 
     def remote(src, dst, send, recv, target):
@@ -88,7 +131,7 @@
         )
 
     def z_copy(i, step):
-        return remote(out_ref.at[i], raw.at[i, mine], z_send.at[i], z_recv.at[i], {"walk": partner(walk, step, walks)})
+        return remote(outgoing.at[i], raw.at[i, mine], z_send.at[i], z_recv.at[i], {"walk": partner(walk, step, walks)})
 
     def x_copy(i, step):
         return remote(raw.at[i, mine], raw.at[i, mine], x_send.at[step, i], x_recv.at[step, i], {"slab": slab_peer(step)})
@@ -112,16 +155,13 @@
         z_copy(i, i // local).start()
     pairs = [
         small(trial_ref, trial, tx_send, tx_recv, tc_send, tc_recv),
-        small(field_ref, field, fx_send, fx_recv, fc_send, fc_recv),
+        small(field_out, field, fx_send, fx_recv, fc_send, fc_recv),
     ]
     for x, c in pairs:
         for step in range(1, slabs):
             x(step).start()
         for step in range(1, cores):
             c(0, step).start()
-    for copy in own:
-        copy.wait()
-
     def spread(i):
         for step in range(1, slabs):
             x_copy(i, step).start()
@@ -189,8 +229,8 @@
         contracted = dot(half[i], inverse[i])
         for g in range(vectors):
             block = contracted[g * electrons : (g + 1) * electrons, :]
-            bias_ref[i, g : g + 1, :] = jnp.sum(jnp.where(diagonal, block, 0.0), axis=0, keepdims=True)
-            exch_ref[i, g : g + 1, :] = jnp.sum(block * jnp.transpose(block), axis=0, keepdims=True)
+            traces[i, g : g + 1, :] = jnp.sum(jnp.where(diagonal, block, 0.0), axis=0, keepdims=True)
+            squares[i, g : g + 1, :] = jnp.sum(block * jnp.transpose(block), axis=0, keepdims=True)
 
     ready = cores + 1
 
@@ -217,7 +257,15 @@
                 if part == 0:
                     first_guess(n)
 
-                @pl.loop(ITERS * part // cores, ITERS * (part + 1) // cores)
+                first, middle, last = ITERS * part // cores, EARLY, ITERS * (part + 1) // cores
+
+                @pl.loop(first, max(first, min(middle, last)))
+                def _(iteration):
+                    both = stack[...]
+                    low = both.astype(jnp.bfloat16)
+                    stack[...] = 2.0 * both - dot(low, low[electrons:, :])
+
+                @pl.loop(min(last, max(middle, first)), last)
                 def _(iteration):
                     both = stack[...]
                     stack[...] = 2.0 * both - dot3(both, both[electrons:, :])
@@ -230,6 +278,18 @@
         @pl.when(i >= ready + cores)
         def _():
             finish(i - ready - cores)
+
+    alive = lax.broadcasted_iota(jnp.int32, bias_ref.shape, 0) < count_ref[0]
+    column = lax.broadcasted_iota(jnp.int32, bias_ref.shape, 1)
+    for terms, rows_of, result, factor in ((traces, bias_rows, bias_ref, 1.0), (squares, exch_rows, exch_ref, -0.5)):
+        for j in range(slots):
+            block = terms[slot_of[j]]
+            for g in range(vectors):
+                rows_of[g, j : j + 1, :] = block[g : g + 1, :]
+        total = jnp.zeros(result.shape, jnp.float32)
+        for g in range(vectors):
+            total = jnp.where(column == g, jnp.sum(rows_of[g], axis=1, keepdims=True), total)
+        result[...] = jnp.where(alive, factor * total, 0.0)
 
     for i in range(local, slots):
         z_copy(i, i // local).wait_send()
@@ -259,45 +319,41 @@
     per_device, rows, electrons = walkers.shape
     vectors = cholesky.shape[0]
     capacity = (per_device + walks - 1) // walks
-    sender = branches.reshape(walks, per_device) // per_device
-    local_index = branches.reshape(walks, per_device) % per_device
-    places = jnp.arange(per_device, dtype=jnp.int32)
-    same_sender = sender[:, :, None] == sender[:, None, :]
-    rank = jnp.sum(same_sender & (places[None, :] < places[:, None])[None], axis=2)
-    my_sender = lax.dynamic_index_in_dim(sender, walk, 0, keepdims=False)
-    my_rank = lax.dynamic_index_in_dim(rank, walk, 0, keepdims=False)
-    full = walks * capacity == per_device
-    wanted = (sender[:, None, :] == walk) & (rank[:, None, :] == jnp.arange(capacity, dtype=jnp.int32)[None, :, None])
-    chosen = jnp.sum(jnp.where(wanted, local_index[:, None, :], 0), axis=2)
-    if full:
-        steps = jnp.arange(walks, dtype=jnp.int32)
-        order = jnp.stack([partner(walk, step, walks) for step in range(walks)])
-        origin = order if walks & (walks - 1) == 0 else (walk - steps) % walks
-        chosen = jnp.sum(jnp.where(order[:, None, None] == steps[None, :, None], chosen[None], 0), axis=1)
-        outgoing = jnp.take(walkers, chosen.reshape(-1), axis=0, mode="clip")
-        step_of = jnp.sum(jnp.where(my_sender[:, None] == origin[None, :], steps[None, :], 0), axis=1)
-        slot = step_of * capacity + my_rank
-        local = capacity
-    else:
+    local = capacity if walks * capacity == per_device else per_device
+    if local == per_device:
+        sender = branches.reshape(walks, per_device) // per_device
+        local_index = branches.reshape(walks, per_device) % per_device
+        places = jnp.arange(per_device, dtype=jnp.int32)
+        same_sender = sender[:, :, None] == sender[:, None, :]
+        rank = jnp.sum(same_sender & (places[None, :] < places[:, None])[None], axis=2)
+        ranks = jnp.arange(capacity, dtype=jnp.int32)[None, :, None]
+        wanted = (sender[:, None, :] == walk) & (rank[:, None, :] == ranks)
+        chosen = jnp.sum(jnp.where(wanted, local_index[:, None, :], 0), axis=2)
         outgoing = jnp.take(walkers, chosen.reshape(-1), axis=0, mode="clip")
         outgoing = outgoing.reshape(walks, capacity, rows, electrons)
         arrived = lax.all_to_all(outgoing, "walk", split_axis=0, concat_axis=0, tiled=True)
         arrived = arrived.reshape(walks * capacity, rows, electrons)
-        outgoing = jnp.take(arrived, my_sender * capacity + my_rank, axis=0, mode="clip")
-        slot = places
-        local = per_device
-    here = slot[:, None] == places[None, :]
-    slot_field = jnp.sum(jnp.where(here[:, :, None], field[:, None, :], 0.0), axis=0)
+        my_sender = lax.dynamic_index_in_dim(sender, walk, 0, keepdims=False)
+        my_rank = lax.dynamic_index_in_dim(rank, walk, 0, keepdims=False)
+        walkers = jnp.take(arrived, my_sender * capacity + my_rank, axis=0, mode="clip")
     shards = slabs * cores
     share = per_device // cores
     dma = pltpu.SemaphoreType.DMA
     vmem = pl.BlockSpec(memory_space=pltpu.VMEM)
-    bias, exchange = pl.pallas_call(
+    return pl.pallas_call(
         functools.partial(kernel, (walks, slabs, cores, per_device, local)),
-        out_shape=[jax.ShapeDtypeStruct((per_device, vectors, electrons), jnp.float32)] * 2,
-        in_specs=[pl.BlockSpec(memory_space=pl.ANY)] * 4,
+        out_shape=[jax.ShapeDtypeStruct((per_device, vectors), jnp.float32)] * 2,
+        in_specs=[pl.BlockSpec(memory_space=pltpu.SMEM)] * 2 + [pl.BlockSpec(memory_space=pl.ANY)] * 4,
         out_specs=[vmem] * 2,
         scratch_shapes=[
+            pltpu.VMEM((per_device, rows, electrons), jnp.bfloat16),
+            pltpu.VMEM((per_device, rows, electrons), jnp.bfloat16),
+            pltpu.VMEM((per_device, rows), jnp.float32),
+            pltpu.VMEM((per_device, rows), jnp.float32),
+            pltpu.VMEM((per_device, vectors, electrons), jnp.float32),
+            pltpu.VMEM((per_device, vectors, electrons), jnp.float32),
+            pltpu.VMEM((vectors, per_device, electrons), jnp.float32),
+            pltpu.VMEM((vectors, per_device, electrons), jnp.float32),
             pltpu.VMEM((per_device, shards, rows, electrons), jnp.bfloat16),
             pltpu.VMEM((shards, electrons, rows), jnp.bfloat16),
             pltpu.VMEM((shards, per_device, rows), jnp.float32),
@@ -313,16 +369,12 @@
             dma((share, cores)), dma((share, cores)),
             dma((slabs,)), dma((slabs,)), dma((slabs, cores)), dma((slabs, cores)),
             dma((slabs,)), dma((slabs,)), dma((slabs, cores)), dma((slabs, cores)),
-            dma((local + 3,)),
+            dma((4,)),
         ],
         compiler_params=pltpu.CompilerParams(
             collective_id=0, has_side_effects=True, vmem_limit_bytes=48 * 1024 * 1024
         ),
-    )(outgoing, trial_orbitals.T, cholesky.reshape(vectors * electrons, shards * rows), slot_field)
-    living = (places < counts[0]).astype(jnp.float32)[:, None]
-    bias = jnp.sum(jnp.where(here[:, :, None], jnp.sum(bias, axis=2)[None], 0.0), axis=1)
-    exchange = jnp.sum(jnp.where(here[:, :, None], jnp.sum(exchange, axis=2)[None], 0.0), axis=1)
-    return bias * living, -0.5 * exchange * living
+    )(branches, counts, walkers, trial_orbitals.T, cholesky.reshape(vectors * electrons, shards * rows), field)
 
 
 def solution(mesh):

time: 56.8 us -> 55.6 us (0.979); the launches traced: 55.9 us -> 55.3 us
  local copies, waits for them, and re-layouts: 2.33 us -> 5.37 us
  other arithmetic: 1.79 us -> 0 us
  Pallas kernels: 50.3 us -> 48.6 us
    unnamed x11 -> x9, local copies, waits for them, and re-layouts: 1.27 us -> 4.1 us
    pallas_call x1, Pallas kernels: 50.3 us -> 48.6 us  [on_device(): pl.pallas_call(functools.partial(kernel, (walks, slabs, cores, per_device...]
    pallas_call x0 -> x2, local copies, waits for them, and re-layouts: none -> 1.27 us  [on_device(): pl.pallas_call(functools.partial(kernel, (walks, slabs, cores, per_device...]
    reduce_sum x8 -> x0, other arithmetic: 0.94 us -> none  [the longest x1 0.21 us: on_device(): jnp.sum(same_sender & (places[None, :] < places[:, None])[None], axis=2)]
    gather x1 -> x0, local copies, waits for them, and re-layouts: 0.61 us -> none  [on_device(): outgoing = jnp.take(walkers, chosen.reshape(-1), axis=0, mode='clip')]
    mul x2 -> x0, other arithmetic: 0.57 us -> none  [on_device(): return (bias * living, -0.5 * exchange * living)]
where the time goes in v3:
time: 55.6 us; the launch traced here: 55.3 us
  Pallas kernels  48.6 us (87%)
  local copies, waits for them, and re-layouts  5.37 us (10%)
  between operations  1.32 us (2%)
    pallas_call x1, Pallas kernels, on_device(): pl.pallas_call(functools.partial(kernel, (walks, slabs, cores, per_device...  48.6 us
    unnamed x9, local copies, waits for them, and re-layouts  4.1 us
    pallas_call x2, local copies, waits for them, and re-layouts, on_device(): pl.pallas_call(functools.partial(kernel, (walks, slabs, cores, per_device...  1.27 us

profile of v3, /device:TPU:1, one launch (start us, length us, event | category | flops | bytes accessed | tf_op | source)
XLA Modules:
  0.0 55.3 jit_solution(12759662144155640552)
XLA Ops:
  1.3 0.0 copy-start.2
  1.3 1.0 %copy.8 = bf16[256,256]{0,1:T(8,128)(2,1)S(1)} copy(bf16[256,256]{1,0:T(8,128)(2,1)} %param.7) | data formatting | bytes 262144 | tf_op args[1]
  2.3 0.0 copy-start.3
  2.3 0.0 copy-done.2
  2.3 0.6 %copy-done.3 = s32[32]{0:T(128)S(1)} copy-done((s32[32]{0:T(128)S(1)}, s32[32]{0:T(128)}, u32[]{:S(2)}) %copy-start.3) | copy-done | bytes 152
  3.0 0.0 copy-start
  3.0 1.2 %copy-done = bf16[8,256,256]{2,1,0:T(8,128)(2,1)S(1)} copy-done((bf16[8,256,256]{2,1,0:T(8,128)(2,1)S(1)}, bf16[8,256,256]{2,1,0:T(8,128)(2,1)}, u32[]{:S(2)}) %copy-start) | copy-done | bytes 1048600
  4.2 0.0 copy-start.1
  4.2 1.2 %copy-done.1 = bf16[2,256,1024]{2,1,0:T(8,128)(2,1)S(1)} copy-done((bf16[2,256,1024]{2,1,0:T(8,128)(2,1)S(1)}, bf16[2,256,1024]{2,1,0:T(8,128)(2,1)}, u32[]{:S(2)}) %copy-start.1) | copy-done | bytes 1048600
  5.4 48.6 %shard_map.77 = (f32[8,2]{1,0:T(8,128)S(1)}, f32[8,2]{1,0:T(8,128)S(1)}) custom-call(s32[32]{0:T(128)S(1)} %copy-done.3, s32[1]{0:T(128)S(6)} %copy.11.count_ref, bf16[8,256,256]{2,1,0:T(8,128)(2,1)S(1)} %copy-done, bf16[256,256]{1,0:T(8,128)(2,1)S(1)} %bitcast.3, bf16[512,1024]{1,0:T(8,128)(2,1)S(1)} %bitcast.2, f32[8,256]{1,0:T(8,128)S(1)} %copy-done.2), custom_call_target="tpu_custom_call" | custom-call | tf_op jit(solution)/shard_map/pallas_call | solution.py:343
  54.0 0.6 %copy.9 = f32[8,2]{0,1:T(2,128)} copy(f32[8,2]{1,0:T(8,128)S(1)} %get-tuple-element.2) | data formatting | bytes 128 | tf_op jit(solution)/shard_map/pallas_call | solution.py:343
  54.7 0.6 %copy.10 = f32[8,2]{0,1:T(2,128)} copy(f32[8,2]{1,0:T(8,128)S(1)} %get-tuple-element.3) | data formatting | bytes 128 | tf_op jit(solution)/shard_map/pallas_call | solution.py:343
Async XLA Ops:
  1.3 1.0 %copy-start.2 = (f32[8,256]{1,0:T(8,128)S(1)}, f32[8,256]{1,0:T(8,128)}, u32[]{:S(2)}) copy-start(f32[8,256]{1,0:T(8,128)} %field_ref.1) | copy-start | bytes 24580
  2.3 0.7 %copy-start.3 = (s32[32]{0:T(128)S(1)}, s32[32]{0:T(128)}, u32[]{:S(2)}) copy-start(s32[32]{0:T(128)} %branch_ref.1) | copy-start | bytes 388
  3.0 1.2 %copy-start = (bf16[8,256,256]{2,1,0:T(8,128)(2,1)S(1)}, bf16[8,256,256]{2,1,0:T(8,128)(2,1)}, u32[]{:S(2)}) copy-start(bf16[8,256,256]{2,1,0:T(8,128)(2,1)} %walker_ref.1) | copy-start | bytes 3145732
  4.2 1.2 %copy-start.1 = (bf16[2,256,1024]{2,1,0:T(8,128)(2,1)S(1)}, bf16[2,256,1024]{2,1,0:T(8,128)(2,1)}, u32[]{:S(2)}) copy-start(bf16[2,256,1024]{2,1,0:T(8,128)(2,1)} %param.8) | copy-start | bytes 3145732

commit v4 on v3

--- a/solution.py
+++ b/solution.py
@@ -40,14 +40,14 @@
 
 
 def kernel(
-    sizes, branch_ref, count_ref, walker_ref, trial_ref, chol_ref, field_ref, bias_ref, exch_ref,
-    source, outgoing, field_in, field_out, traces, squares, bias_rows, exch_rows, raw, trial, field, chol, prop, half, inter, stack, inverse,
+    sizes, branch_in, walker_ref, trial_ref, chol_ref, field_ref, bias_ref, exch_ref,
+    branch_ref, trial_t, source, outgoing, field_in, field_out, traces, squares, bias_rows, exch_rows, raw, trial, field, chol, prop, half, inter, stack, inverse,
     z_send, z_recv, x_send, x_recv, c_send, c_recv, i_send, i_recv,
     tx_send, tx_recv, tc_send, tc_recv, fx_send, fx_recv, fc_send, fc_recv, own_sem,
 ):
     walks, slabs, cores, slots, local = sizes
     walk, slab, core = lax.axis_index("walk"), lax.axis_index("slab"), lax.axis_index("row")
-    rows, electrons = trial_ref.shape[1], trial_ref.shape[0]
+    rows, electrons = trial_ref.shape
     vectors = chol_ref.shape[0] // electrons
     mine = slab * cores + core
 
@@ -63,7 +63,7 @@
     def core_source(step):
         return lax.rem(core + cores - step, cores)
 
-    loads = [(walker_ref, source), (field_ref, field_in), (trial_ref, trial.at[mine]), (chol_ref, chol)]
+    loads = [(branch_in, branch_ref), (walker_ref, source), (field_ref, field_in), (trial_ref, trial.at[mine]), (chol_ref, chol)]
     own = [pltpu.make_async_copy(src, dst, own_sem.at[k]) for k, (src, dst) in enumerate(loads)]
     for copy in own:
         copy.start()
@@ -91,7 +91,7 @@
             count = count + jnp.where(hit, 1, 0)
         return picks
 
-    for copy in own[:2]:
+    for copy in own[:3]:
         copy.wait()
     slot_of = list(range(slots))
     if local < slots:
@@ -121,7 +121,7 @@
             raw[i, mine] = source[i]
         field_out[...] = field_in[...]
     field[mine] = field_out[...]
-    for copy in own[2:]:
+    for copy in own[3:]:
         copy.wait()
     pl.semaphore_wait(barrier, greeted)
 
@@ -183,14 +183,14 @@
             lane = lax.broadcasted_iota(jnp.int32, column.shape, 1)
             scale = jnp.sum(jnp.where(lane == i, column, 0.0), axis=1, keepdims=True)
             prop[q * rows : (q + 1) * rows, :] = (raw[i, q].astype(jnp.float32) * scale).astype(jnp.bfloat16)
+        @pl.when(lax.rem(i, cores) == core)
+        def _():
+            total = dot(trial_t[0], prop[0:rows, :])
+            for q in range(1, slabs * cores):
+                total += dot(trial_t[q], prop[q * rows : (q + 1) * rows, :])
+            inter[i // cores] = total
+
         half[i] = dot(chol[...], prop[...]).astype(jnp.bfloat16)
-
-        @pl.when(lax.rem(i, cores) == core)
-        def _():
-            total = dot(trial[0], prop[0:rows, :])
-            for q in range(1, slabs * cores):
-                total += dot(trial[q], prop[q * rows : (q + 1) * rows, :])
-            inter[i // cores] = total
 
     for i in range(local):
         spread(i)
@@ -204,6 +204,8 @@
             for step in range(1, cores):
                 c(hop, step).wait_recv()
 
+    for q in range(slabs * cores):
+        trial_t[q] = jnp.transpose(trial[q].astype(jnp.float32)).astype(jnp.bfloat16)
     share = slots // cores
     line = lax.broadcasted_iota(jnp.int32, (electrons, electrons), 0)
     diagonal = line == lax.broadcasted_iota(jnp.int32, (electrons, electrons), 1)
@@ -234,16 +236,12 @@
 
     ready = cores + 1
 
-    @pl.loop(0, slots + ready + cores)
+    @pl.loop(0, slots + ready + cores + 1)
     def _(i):
         @pl.when((i >= local) & (i < slots))
         def _():
             z_copy(i, 0).wait_recv()
             spread(i)
-
-        @pl.when((i > 0) & (i <= slots))
-        def _():
-            relay(i - 1)
 
         @pl.when((i > 1) & (i < slots + 2))
         def _():
@@ -275,13 +273,16 @@
                     for step in range(1, cores):
                         i_copy(n * cores + core, step).start()
 
-        @pl.when(i >= ready + cores)
-        def _():
-            finish(i - ready - cores)
-
-    alive = lax.broadcasted_iota(jnp.int32, bias_ref.shape, 0) < count_ref[0]
+        @pl.when(i > ready + cores)
+        def _():
+            finish(i - ready - cores - 1)
+
+        @pl.when((i > 0) & (i <= slots))
+        def _():
+            relay(i - 1)
+
     column = lax.broadcasted_iota(jnp.int32, bias_ref.shape, 1)
-    for terms, rows_of, result, factor in ((traces, bias_rows, bias_ref, 1.0), (squares, exch_rows, exch_ref, -0.5)):
+    for terms, rows_of, result in ((traces, bias_rows, bias_ref), (squares, exch_rows, exch_ref)):
         for j in range(slots):
             block = terms[slot_of[j]]
             for g in range(vectors):
@@ -289,7 +290,7 @@
         total = jnp.zeros(result.shape, jnp.float32)
         for g in range(vectors):
             total = jnp.where(column == g, jnp.sum(rows_of[g], axis=1, keepdims=True), total)
-        result[...] = jnp.where(alive, factor * total, 0.0)
+        result[...] = total
 
     for i in range(local, slots):
         z_copy(i, i // local).wait_send()
@@ -340,12 +341,14 @@
     share = per_device // cores
     dma = pltpu.SemaphoreType.DMA
     vmem = pl.BlockSpec(memory_space=pltpu.VMEM)
-    return pl.pallas_call(
+    bias, exchange = pl.pallas_call(
         functools.partial(kernel, (walks, slabs, cores, per_device, local)),
         out_shape=[jax.ShapeDtypeStruct((per_device, vectors), jnp.float32)] * 2,
-        in_specs=[pl.BlockSpec(memory_space=pltpu.SMEM)] * 2 + [pl.BlockSpec(memory_space=pl.ANY)] * 4,
+        in_specs=[pl.BlockSpec(memory_space=pl.ANY)] * 5,
         out_specs=[vmem] * 2,
         scratch_shapes=[
+            pltpu.SMEM(branches.shape, jnp.int32),
+            pltpu.VMEM((shards, electrons, rows), jnp.bfloat16),
             pltpu.VMEM((per_device, rows, electrons), jnp.bfloat16),
             pltpu.VMEM((per_device, rows, electrons), jnp.bfloat16),
             pltpu.VMEM((per_device, rows), jnp.float32),
@@ -355,7 +358,7 @@
             pltpu.VMEM((vectors, per_device, electrons), jnp.float32),
             pltpu.VMEM((vectors, per_device, electrons), jnp.float32),
             pltpu.VMEM((per_device, shards, rows, electrons), jnp.bfloat16),
-            pltpu.VMEM((shards, electrons, rows), jnp.bfloat16),
+            pltpu.VMEM((shards, rows, electrons), jnp.bfloat16),
             pltpu.VMEM((shards, per_device, rows), jnp.float32),
             pltpu.VMEM((vectors * electrons, shards * rows), jnp.bfloat16),
             pltpu.VMEM((shards * rows, electrons), jnp.bfloat16),
@@ -369,12 +372,14 @@
             dma((share, cores)), dma((share, cores)),
             dma((slabs,)), dma((slabs,)), dma((slabs, cores)), dma((slabs, cores)),
             dma((slabs,)), dma((slabs,)), dma((slabs, cores)), dma((slabs, cores)),
-            dma((4,)),
+            dma((5,)),
         ],
         compiler_params=pltpu.CompilerParams(
             collective_id=0, has_side_effects=True, vmem_limit_bytes=48 * 1024 * 1024
         ),
-    )(branches, counts, walkers, trial_orbitals.T, cholesky.reshape(vectors * electrons, shards * rows), field)
+    )(branches, walkers, trial_orbitals, cholesky.reshape(vectors * electrons, shards * rows), field)
+    living = (jnp.arange(per_device, dtype=jnp.int32) < counts[0]).astype(jnp.float32)[:, None]
+    return bias * living, -0.5 * exchange * living
 
 
 def solution(mesh):

time: 55.6 us -> 58 us (1.043)
  Pallas kernels: 48.6 us -> 51.1 us
    pallas_call x1, Pallas kernels: 48.6 us -> 51.1 us  [on_device(): pl.pallas_call(functools.partial(kernel, (walks, slabs, cores, per_device...]
    pallas_call x2 -> x0, local copies, waits for them, and re-layouts: 1.27 us -> none  [on_device(): pl.pallas_call(functools.partial(kernel, (walks, slabs, cores, per_device...]
    unnamed x9 -> x12, local copies, waits for them, and re-layouts: 4.1 us -> 5.26 us
where the time goes in v4:
time: 58 us; the launch traced here: 57.7 us
  Pallas kernels  51.1 us (88%)
  local copies, waits for them, and re-layouts  5.26 us (9%)
  between operations  1.34 us (2%)
    pallas_call x1, Pallas kernels, on_device(): pl.pallas_call(functools.partial(kernel, (walks, slabs, cores, per_device...  51.1 us
    unnamed x12, local copies, waits for them, and re-layouts  5.26 us

profile of v4, /device:TPU:1, one launch (start us, length us, event | category | flops | bytes accessed | tf_op | source)
XLA Modules:
  0.0 57.7 jit_solution(13166566788915946546)
XLA Ops:
  0.6 0.0 copy-start.3
  1.3 0.0 copy-start.4
  1.3 0.0 copy-done.3
  1.3 0.6 %copy-done.4 = s32[32]{0:T(128)S(1)} copy-done((s32[32]{0:T(128)S(1)}, s32[32]{0:T(128)}, u32[]{:S(2)}) %copy-start.4) | copy-done | bytes 152
  2.0 0.0 copy-start
  2.0 1.2 %copy-done = bf16[8,256,256]{2,1,0:T(8,128)(2,1)S(1)} copy-done((bf16[8,256,256]{2,1,0:T(8,128)(2,1)S(1)}, bf16[8,256,256]{2,1,0:T(8,128)(2,1)}, u32[]{:S(2)}) %copy-start) | copy-done | bytes 1048600
  3.2 0.0 copy-start.1
  3.2 1.2 %copy-done.1 = bf16[2,256,1024]{2,1,0:T(8,128)(2,1)S(1)} copy-done((bf16[2,256,1024]{2,1,0:T(8,128)(2,1)S(1)}, bf16[2,256,1024]{2,1,0:T(8,128)(2,1)}, u32[]{:S(2)}) %copy-start.1) | copy-done | bytes 1048600
  4.4 0.0 copy-start.2
  4.4 0.9 %copy-done.2 = bf16[256,256]{1,0:T(8,128)(2,1)S(1)} copy-done((bf16[256,256]{1,0:T(8,128)(2,1)S(1)}, bf16[256,256]{1,0:T(8,128)(2,1)}, u32[]{:S(2)}) %copy-start.2) | copy-done | bytes 131096
  5.3 51.1 %shard_map.77 = (f32[8,2]{1,0:T(8,128)S(1)}, f32[8,2]{1,0:T(8,128)S(1)}) custom-call(s32[32]{0:T(128)S(1)} %copy-done.4, bf16[8,256,256]{2,1,0:T(8,128)(2,1)S(1)} %copy-done, bf16[256,256]{1,0:T(8,128)(2,1)S(1)} %copy-done.2, bf16[512,1024]{1,0:T(8,128)(2,1)S(1)} %bitcast.4, f32[8,256]{1,0:T(8,128)S(1)} %copy-done.3), custom_call_target="tpu_custom_call" | custom-call | tf_op jit(solution)/shard_map/pallas_call | solution.py:344
  56.4 0.1 broadcast_multiply_fusion
  56.5 0.6 %copy.9 = f32[8,2]{0,1:T(2,128)} copy(f32[8,2]{1,0:T(8,128)S(1)} %get-tuple-element.8) | data formatting | bytes 128
  57.1 0.6 %copy.8 = f32[8,2]{0,1:T(2,128)} copy(f32[8,2]{1,0:T(8,128)S(1)} %get-tuple-element.9) | data formatting | bytes 128
  (2 shorter events, 0.0 us)
Async XLA Ops:
  0.6 0.7 %copy-start.3 = (f32[8,256]{1,0:T(8,128)S(1)}, f32[8,256]{1,0:T(8,128)}, u32[]{:S(2)}) copy-start(f32[8,256]{1,0:T(8,128)} %field_ref.1) | copy-start | bytes 24580
  1.3 0.7 %copy-start.4 = (s32[32]{0:T(128)S(1)}, s32[32]{0:T(128)}, u32[]{:S(2)}) copy-start(s32[32]{0:T(128)} %branch_in.1) | copy-start | bytes 388
  2.0 1.2 %copy-start = (bf16[8,256,256]{2,1,0:T(8,128)(2,1)S(1)}, bf16[8,256,256]{2,1,0:T(8,128)(2,1)}, u32[]{:S(2)}) copy-start(bf16[8,256,256]{2,1,0:T(8,128)(2,1)} %walker_ref.1) | copy-start | bytes 3145732
  3.2 1.2 %copy-start.1 = (bf16[2,256,1024]{2,1,0:T(8,128)(2,1)S(1)}, bf16[2,256,1024]{2,1,0:T(8,128)(2,1)}, u32[]{:S(2)}) copy-start(bf16[2,256,1024]{2,1,0:T(8,128)(2,1)} %param.8) | copy-start | bytes 3145732
  4.4 0.9 %copy-start.2 = (bf16[256,256]{1,0:T(8,128)(2,1)S(1)}, bf16[256,256]{1,0:T(8,128)(2,1)}, u32[]{:S(2)}) copy-start(bf16[256,256]{1,0:T(8,128)(2,1)} %trial_ref.1) | copy-start | bytes 393220

commit v5 on v4

--- a/solution.py
+++ b/solution.py
@@ -247,6 +247,10 @@
         def _():
             compute(i - 2)
 
+        @pl.when((i > 0) & (i <= slots))
+        def _():
+            relay(i - 1)
+
         for part in range(cores):
 
             @pl.when((i >= ready) & (i < slots + ready) & (lax.rem(i + cores - 1, cores) == part))
@@ -277,9 +281,6 @@
         def _():
             finish(i - ready - cores - 1)
 
-        @pl.when((i > 0) & (i <= slots))
-        def _():
-            relay(i - 1)
 
     column = lax.broadcasted_iota(jnp.int32, bias_ref.shape, 1)
     for terms, rows_of, result in ((traces, bias_rows, bias_ref), (squares, exch_rows, exch_ref)):
@@ -375,7 +376,7 @@
             dma((5,)),
         ],
         compiler_params=pltpu.CompilerParams(
-            collective_id=0, has_side_effects=True, vmem_limit_bytes=48 * 1024 * 1024
+            collective_id=0, has_side_effects=True, vmem_limit_bytes=63 * 1024 * 1024
         ),
     )(branches, walkers, trial_orbitals, cholesky.reshape(vectors * electrons, shards * rows), field)
     living = (jnp.arange(per_device, dtype=jnp.int32) < counts[0]).astype(jnp.float32)[:, None]

time: 58 us -> 49.4 us (0.85)
  Pallas kernels: 51.1 us -> 45.8 us
  local copies, waits for them, and re-layouts: 5.26 us -> 1.27 us
  other arithmetic: 0.08 us -> 0.76 us
    pallas_call x1, Pallas kernels: 51.1 us -> 45.8 us  [on_device(): pl.pallas_call(functools.partial(kernel, (walks, slabs, cores, per_device...]
    unnamed x12 -> x2, local copies, waits for them, and re-layouts: 5.26 us -> 1.27 us
    mul x2, other arithmetic: 0.08 us -> 0.76 us  [on_device(): return (bias * living, -0.5 * exchange * living)]
where the time goes in v5:
time: 49.4 us; the launch traced here: 49.2 us
  Pallas kernels  45.8 us (93%)
  between operations  1.3 us (3%)
  local copies, waits for them, and re-layouts  1.27 us (3%)
  other arithmetic  0.76 us (2%)
    pallas_call x1, Pallas kernels, on_device(): pl.pallas_call(functools.partial(kernel, (walks, slabs, cores, per_device...  45.8 us
    unnamed x2, local copies, waits for them, and re-layouts  1.27 us

profile of v5, /device:TPU:1, one launch (start us, length us, event | category | flops | bytes accessed | tf_op | source)
XLA Modules:
  0.0 49.2 jit_solution(2029062016556997710)
XLA Ops:
  1.3 45.8 %shard_map.77 = (f32[8,2]{1,0:T(8,128)}, f32[8,2]{1,0:T(8,128)}) custom-call(s32[32]{0:T(128)} %branch_in.1, bf16[8,256,256]{2,1,0:T(8,128)(2,1)} %walker_ref.1, bf16[256,256]{1,0:T(8,128)(2,1)} %trial_ref.1, bf16[512,1024]{1,0:T(8,128)(2,1)} %bitcast.4, f32[8,256]{1,0:T(8,128)} %field_ref.1), custom_call_target="tpu_custom_call" | custom-call | tf_op jit(solution)/shard_map/pallas_call | solution.py:345
  47.1 0.8 %broadcast_multiply_fusion = (f32[8,2]{1,0:T(8,128)S(1)}, f32[8,2]{1,0:T(8,128)S(1)}) fusion(f32[8,2]{1,0:T(8,128)} %get-tuple-element.5, f32[8]{0:T(128)S(1)} %compare_select_fusion, f32[8,2]{1,0:T(8,128)} %get-tuple-element.4, f32[8]{0:T(128)S(1)} %compare_convert_fusion), kind=kLoop, calls=%fused_computation | loop fusion | flops 32 | bytes 320 | tf_op jit(solution)/shard_map/mul | solution.py:383
  47.9 0.6 %copy.9 = f32[8,2]{0,1:T(2,128)} copy(f32[8,2]{1,0:T(8,128)S(1)} %get-tuple-element.8) | data formatting | bytes 128
  48.5 0.6 %copy.8 = f32[8,2]{0,1:T(2,128)} copy(f32[8,2]{1,0:T(8,128)S(1)} %get-tuple-element.9) | data formatting | bytes 128
  (2 shorter events, 0.0 us)

commit v6 on v5

--- a/solution.py
+++ b/solution.py
@@ -238,10 +238,10 @@
 
     @pl.loop(0, slots + ready + cores + 1)
     def _(i):
-        @pl.when((i >= local) & (i < slots))
-        def _():
-            z_copy(i, 0).wait_recv()
-            spread(i)
+        @pl.when((i >= local - 1) & (i < slots - 1))
+        def _():
+            z_copy(i + 1, 0).wait_recv()
+            spread(i + 1)
 
         @pl.when((i > 1) & (i < slots + 2))
         def _():

time: 49.4 us -> 50 us (1.012)
  Pallas kernels: 45.8 us -> 46.5 us
    pallas_call x1, Pallas kernels: 45.8 us -> 46.5 us  [on_device(): pl.pallas_call(functools.partial(kernel, (walks, slabs, cores, per_device...]
where the time goes in v6:
time: 50 us; the launch traced here: 49.8 us
  Pallas kernels  46.5 us (93%)
  between operations  1.3 us (3%)
  local copies, waits for them, and re-layouts  1.27 us (3%)
  other arithmetic  0.76 us (2%)
    pallas_call x1, Pallas kernels, on_device(): pl.pallas_call(functools.partial(kernel, (walks, slabs, cores, per_device...  46.5 us
    unnamed x2, local copies, waits for them, and re-layouts  1.27 us

profile of v6, /device:TPU:1, one launch (start us, length us, event | category | flops | bytes accessed | tf_op | source)
XLA Modules:
  0.0 49.8 jit_solution(11163544555798104581)
XLA Ops:
  1.3 46.5 %shard_map.77 = (f32[8,2]{1,0:T(8,128)}, f32[8,2]{1,0:T(8,128)}) custom-call(s32[32]{0:T(128)} %branch_in.1, bf16[8,256,256]{2,1,0:T(8,128)(2,1)} %walker_ref.1, bf16[256,256]{1,0:T(8,128)(2,1)} %trial_ref.1, bf16[512,1024]{1,0:T(8,128)(2,1)} %bitcast.4, f32[8,256]{1,0:T(8,128)} %field_ref.1), custom_call_target="tpu_custom_call" | custom-call | tf_op jit(solution)/shard_map/pallas_call | solution.py:345
  47.8 0.8 %broadcast_multiply_fusion = (f32[8,2]{1,0:T(8,128)S(1)}, f32[8,2]{1,0:T(8,128)S(1)}) fusion(f32[8,2]{1,0:T(8,128)} %get-tuple-element.5, f32[8]{0:T(128)S(1)} %compare_select_fusion, f32[8,2]{1,0:T(8,128)} %get-tuple-element.4, f32[8]{0:T(128)S(1)} %compare_convert_fusion), kind=kLoop, calls=%fused_computation | loop fusion | flops 32 | bytes 320 | tf_op jit(solution)/shard_map/mul | solution.py:383
  48.5 0.6 %copy.9 = f32[8,2]{0,1:T(2,128)} copy(f32[8,2]{1,0:T(8,128)S(1)} %get-tuple-element.8) | data formatting | bytes 128
  49.2 0.6 %copy.8 = f32[8,2]{0,1:T(2,128)} copy(f32[8,2]{1,0:T(8,128)S(1)} %get-tuple-element.9) | data formatting | bytes 128
  (2 shorter events, 0.0 us)
